TPU v7x, 512 devices: a whole 4x8x8 slice. The times are simulated.
512 devices in a mesh: row: 16 (over x, y_hi), col: 32 (over z, y_lo, core).
Axes of the slice: x: 4, y: 8 (y_hi: 4, y_lo: 2; y = y_hi * 2 + y_lo), z: 8, core: 2. Of those that a mesh axis runs over, the one named last changes fastest.
Arguments:
- left_factor: float32 [8192, 512], P(('row', 'col')), may hold values from -0.0625 to 0.0625
- left_cotangent: float32 [8192, 512], P(('row', 'col')), may hold values from -80 to 80
- right_factor: float32 [24576, 512], P(('col', 'row')), may hold values from -0.0390625 to 0.0390625
- right_cotangent: float32 [24576, 512], P(('col', 'row')), may hold values from -80 to 80
- singular: float32 [512], replicated, may hold values from 0.5 to 2, as said below
- singular_cotangent: float32 [512], replicated, may hold values from -384 to 384
Outputs:
- matrix_cotangent: float32 [8192, 24576], P('row', 'col')
Inputs may be any that keep to these rules, and one draw needn't show every extreme that they name: `singular`: strictly decreasing; consecutive values differ by at least 0.75 / 512.
All inputs are finite; a program needn't handle non-finite values.
Results may differ from a plain program's by a relative error of at most 0.0003.
Values sent between devices are 32-bit elements; how exact they have to be, the bound alone decides.
No kernel may reach another device: no remote copies, remote signals or barrier semaphores. Data moves between devices by JAX's collectives and lax.ppermute only.
A program may use at most 64 MiB of HBM per device.

v0:
```python
import jax
import jax.numpy as jnp
from jax import lax
from jax.sharding import Mesh
from jax.sharding import PartitionSpec as P

ROW = ("x", "yh")
COL = ("z", "yl", "core")
ALL = ROW + COL
SIZES = (4, 4, 8, 2, 2)
HIGHEST = lax.Precision.HIGHEST


def dot(a, b, contract):
    return lax.dot_general(
        a, b, (contract, ((), ())), precision=HIGHEST, preferred_element_type=jnp.float32
    )


def gather(block, axis, size):
    copies = jnp.broadcast_to(block[None], (size,) + block.shape)
    return lax.all_to_all(copies, axis, 0, 0)


def partial_core(left, left_cot, right, right_cot, singular):
    squares = singular * singular
    spread = squares[None, :] - squares[:, None]
    size_k = singular.shape[0]
    diagonal = jnp.eye(size_k, dtype=jnp.bool_)
    divided = jnp.where(
        diagonal, jnp.float32(0.0), 1.0 / jnp.where(diagonal, jnp.float32(1.0), spread)
    )
    inverse = 1.0 / singular
    rows = ((0,), (0,))
    gram_left = dot(left, left_cot, rows)
    gram_left_t = dot(left_cot, left, rows)
    gram_right = dot(right, right_cot, rows)
    gram_right_t = dot(right_cot, right, rows)
    core = divided * (gram_left - gram_left_t) * singular[None, :]
    core = core + singular[:, None] * (divided * (gram_right - gram_right_t))
    return core - gram_left * inverse[None, :] - inverse[:, None] * gram_right_t


def local(left, left_cot, right, right_cot, singular, singular_cot):
    size_k = singular.shape[0]
    inverse = 1.0 / singular
    n_all = 512
    mine = partial_core(left, left_cot, right, right_cot, singular)
    spread_out = lax.all_to_all(mine.reshape(n_all, 4, 128), ALL, 0, 0)
    left_pair = jnp.concatenate([left, left_cot * inverse[None, :]], axis=1)
    right_pair = jnp.concatenate([right_cot * inverse[None, :], right], axis=1)
    lefts = lax.all_gather(left_pair, COL, axis=0, tiled=True)
    rights = lax.all_gather(right_pair, ROW, axis=0, tiled=True)
    row = jnp.sum(spread_out, axis=0)
    core = gather(row, ALL, n_all).reshape(size_k, size_k) + jnp.diag(singular_cot)
    last = ((1,), (1,))
    flat = dot(lefts, rights, last)
    panel = dot(lefts[:, :size_k], core, ((1,), (0,)))
    return flat + dot(panel, rights[:, size_k:], last)


def solution(mesh):
    fine = Mesh(mesh.devices.reshape(SIZES), ALL)
    placed = (
        P(ROW + COL, None),
        P(ROW + COL, None),
        P(COL + ROW, None),
        P(COL + ROW, None),
        P(),
        P(),
    )
    return jax.shard_map(local, mesh=fine, in_specs=placed, out_specs=P(ROW, COL), check_vma=False)
```

profile of v0, /device:TPU:1, one launch (start us, length us, event | category | flops | bytes accessed | tf_op | source)
XLA Modules:
  0.0 213.5 jit_solution(7543045240568604852)
XLA Ops:
  6.5 0.0 all-gather.3.cloned.1.call-start
  6.5 0.7 broadcast_divide_fusion
  7.3 0.8 broadcast_multiply_fusion.1
  8.1 1.4 pad_maximum_fusion.1
  9.5 0.0 all-gather.3.cloned.1.call-update
  9.5 0.0 all-gather.5.cloned.1.call-start
  9.5 0.9 broadcast_multiply_fusion
  10.4 1.6 pad_maximum_fusion
  12.0 0.0 all-gather.5.cloned.1.call-update
  12.1 1.8 fusion.11
  13.9 0.0 copy-done.2
  13.9 0.0 copy-done.3
  13.9 1.0 fusion.12
  14.9 0.0 copy-done.7
  14.9 0.0 copy-start.4
  14.9 0.0 copy-start.5
  14.9 1.1 fusion.8
  16.1 0.0 copy-done.4
  16.1 1.4 fusion.6
  17.5 0.4 copy.7
  17.9 55.0 %all_to_all.10 = f32[512,4,128]{2,1,0:T(4,128)S(1)} all-to-all(f32[512,4,128]{2,1,0:T(4,128)S(1)} %copy.7), channel_id=1, replica_groups=mesh['x'=4,'yh'=4,'z'=8,'yl'=2,'core'=2] {'x','yh','z','yl','core'}, dimensions={0} | all-to-all | bytes 2097152 | tf_op jit(solution)/shard_map/all_to_all | solution.py:49
  72.9 0.5 reduce_sum.9
  73.5 0.1 broadcast_in_dim.36
  73.6 0.0 copy-start.6
  73.6 42.8 %all_to_all.11 = f32[512,4,128]{2,1,0:T(4,128)S(1)} all-to-all(f32[512,4,128]{2,1,0:T(4,128)S(1)} %broadcast_in_dim.36), channel_id=1, replica_groups=mesh['x'=4,'yh'=4,'z'=8,'yl'=2,'core'=2] {'x','yh','z','yl','core'}, dimensions={0} | all-to-all | bytes 2097152 | tf_op jit(solution)/shard_map/all_to_all | solution.py:22
  116.4 0.4 copy.8
  116.8 0.1 bitcast_add_fusion
  116.9 0.0 all-gather.3.cloned.1.call-done
  116.9 4.2 %fusion.9 = f32[512,512]{1,0:T(8,128)} fusion(f32[512,512]{0,1:T(8,128)S(1)} %bitcast_add_fusion, f32[512,1024]{1,0:T(8,128)} %all-gather.3.cloned.1.call-done), kind=kOutput, calls=%fused_computation.12 | convolution fusion | flops 1610612736 | bytes 3145728 | tf_op jit(solution)/shard_map/dot_general | solution.py:15
  121.1 74.3 %all-gather.5.cloned.1.call-done = f32[768,1024]{1,0:T(8,128)} async-done(((f32[48,1024]{1,0:T(8,128)}), f32[768,1024]{1,0:T(8,128)}) %all-gather.5.cloned.1.call-update) | async-done | bytes 3145744 | tf_op jit(solution)/shard_map/all_gather | solution.py:53
  195.4 4.6 %fusion = f32[512,768]{1,0:T(8,128)S(1)} fusion(f32[512,512]{1,0:T(8,128)} %fusion.9, f32[768,1024]{1,0:T(8,128)} %all-gather.5.cloned.1.call-done), kind=kOutput, calls=%fused_computation | convolution fusion | flops 2415919104 | bytes 4194304 | tf_op jit(solution)/shard_map/dot_general | solution.py:15
  200.1 6.5 %convolution_add_fusion = f32[512,768]{1,0:T(8,128)} fusion(f32[512,768]{1,0:T(8,128)S(1)} %fusion, f32[512,1024]{1,0:T(8,128)S(1)} %copy-done.1, f32[768,1024]{1,0:T(8,128)S(1)} %copy-done), kind=kOutput, calls=%fused_computation.2 | convolution fusion | flops 4832231424 | bytes 8388608 | tf_op jit(solution)/shard_map/dot_general | solution.py:15
  (9 shorter events, 0.0 us)
Async XLA Ops:
  6.5 8.4 %copy-start.7 = (f32[512]{0:T(512)S(1)}, f32[512]{0:T(512)}, u32[]{:S(2)}) copy-start(f32[512]{0:T(512)} %param.10) | copy-start | bytes 6148
  6.5 7.3 %copy-start.2 = (f32[48,512]{1,0:T(8,128)S(1)}, f32[48,512]{1,0:T(8,128)}, u32[]{:S(2)}) copy-start(f32[48,512]{1,0:T(8,128)} %param.9) | copy-start | bytes 294916
  6.5 7.3 %copy-start.3 = (f32[48,512]{1,0:T(8,128)S(1)}, f32[48,512]{1,0:T(8,128)}, u32[]{:S(2)}) copy-start(f32[48,512]{1,0:T(8,128)} %param.8) | copy-start | bytes 294916
  6.5 110.3 %all-gather.3.cloned.1.call-start = ((), (), s32[]{:S(2)}) async-start(), calls=%async_computation.2 | async-start | bytes 2162688 | tf_op jit(solution)/shard_map/all_gather | solution.py:52
  9.5 186.0 %all-gather.5.cloned.1.call-start = ((), (), s32[]{:S(2)}) async-start(), calls=%async_computation.3 | async-start | bytes 3342336 | tf_op jit(solution)/shard_map/all_gather | solution.py:53
  14.9 1.2 copy-start.4
  14.9 1.2 copy-start.5
  73.6 43.2 %copy-start.6 = (f32[512]{0:T(512)S(1)}, f32[512]{0:T(512)}, u32[]{:S(2)}) copy-start(f32[512]{0:T(512)} %param.11) | copy-start | bytes 6148
  116.9 83.2 %copy-start.1 = (f32[512,1024]{1,0:T(8,128)S(1)}, f32[512,1024]{1,0:T(8,128)}, u32[]{:S(2)}) copy-start(f32[512,1024]{1,0:T(8,128)} %all-gather.3.cloned.1.call-done) | copy-start | bytes 6291460
  195.4 4.6 %copy-start = (f32[768,1024]{1,0:T(8,128)S(1)}, f32[768,1024]{1,0:T(8,128)}, u32[]{:S(2)}) copy-start(f32[768,1024]{1,0:T(8,128)} %all-gather.5.cloned.1.call-done) | copy-start | bytes 9437188
Sparse Core Ops, SparseCore 0:
  9.6 101.7 all-gather.2
  114.4 80.9 all-gather.4
where the time goes:
time: 214 us; the launch traced here: 213 us
  blocking collectives  97.8 us (46%)
  waiting for transfers between devices  74.4 us (35%)
  matrix products  20.7 us (10%)
  between operations  13.6 us (6%)
  other arithmetic  6.06 us (3%)
    all_gather x1, waiting for transfers between devices, local(): rights = lax.all_gather(right_pair, ROW, axis=0, tiled=True)  74.3 us
    all_to_all x1, blocking collectives, local(): spread_out = lax.all_to_all(mine.reshape(n_all, 4, 128), ALL, 0, 0)  55 us
    all_to_all x1, blocking collectives, gather(): return lax.all_to_all(copies, axis, 0, 0)  42.8 us
    dot_general x7, matrix products, dot(): lax.dot_general(a, b, (contract, ((), ())), precision=HIGHEST, preferred_...  20.7 us
  transfers between devices with their start and end apart: 2, of which 1 were waited for; matrix products, arithmetic and copies ran while one was open for 6% of the time, Pallas kernels for 0%

commit v1 on v0

--- a/solution.py
+++ b/solution.py
@@ -9,6 +9,9 @@
 ALL = ROW + COL
 SIZES = (4, 4, 8, 2, 2)
 HIGHEST = lax.Precision.HIGHEST
+lead_the_threads = lambda xin: jnp.concatenate(
+    jax.lax.all_to_all(jnp.stack([xin for _ in range(jax.lax.axis_size(ROW))]), ROW, 0, 0), axis=0
+)
 
 
 def dot(a, b, contract):
@@ -50,7 +53,7 @@
     left_pair = jnp.concatenate([left, left_cot * inverse[None, :]], axis=1)
     right_pair = jnp.concatenate([right_cot * inverse[None, :], right], axis=1)
     lefts = lax.all_gather(left_pair, COL, axis=0, tiled=True)
-    rights = lax.all_gather(right_pair, ROW, axis=0, tiled=True)
+    rights = lead_the_threads(right_pair)
     row = jnp.sum(spread_out, axis=0)
     core = gather(row, ALL, n_all).reshape(size_k, size_k) + jnp.diag(singular_cot)
     last = ((1,), (1,))

time: 214 us -> 227 us (1.061)
  the two profiles are of different devices: /device:TPU:1 before, /device:TPU:39 now
where the time goes in v1:
time: 227 us
  waiting for transfers between devices  110 us (48%)
  blocking collectives  48.2 us (21%)
  starting transfers between devices  23.6 us (10%)
  matrix products  21.6 us (10%)
  between operations  13.6 us (6%)
  local copies, waits for them, and re-layouts  6.12 us (3%)
  other arithmetic  4.21 us (2%)
    all_gather x1, waiting for transfers between devices, local(): lefts = lax.all_gather(left_pair, COL, axis=0, tiled=True)  82.3 us
    all_to_all x1, blocking collectives, local(): spread_out = lax.all_to_all(mine.reshape(n_all, 4, 128), ALL, 0, 0)  48.2 us
    all_to_all x1, waiting for transfers between devices, gather(): return lax.all_to_all(copies, axis, 0, 0)  27.2 us
    dot_general x7, matrix products, dot(): lax.dot_general(a, b, (contract, ((), ())), precision=HIGHEST, preferred_...  21.6 us
    all_to_all x1, starting transfers between devices, gather(): return lax.all_to_all(copies, axis, 0, 0)  14.6 us
    all_to_all x1, starting transfers between devices, jax.lax.all_to_all(jnp.stack([xin for _ in range(jax.lax.axis_size(ROW))]...  8.78 us
  transfers between devices with their start and end apart: 3, of which 2 were waited for; matrix products, arithmetic and copies ran while one was open for 4% of the time, Pallas kernels for 0%

profile of v1, /device:TPU:39, one launch (start us, length us, event | category | flops | bytes accessed | tf_op | source)
XLA Modules:
  0.0 226.8 jit_solution(17379407837280669617)
XLA Ops:
  6.5 0.7 broadcast_divide_fusion
  7.2 2.0 fusion.12
  9.2 0.0 copy-start.4
  9.2 0.0 copy-start.5
  9.2 0.0 copy-start.7
  9.2 2.1 fusion.8
  11.3 0.0 copy-done.4
  11.4 0.0 copy-done.5
  11.4 1.0 fusion.11
  12.4 0.0 copy-done.7
  12.4 1.4 fusion.6
  13.8 0.4 copy.7
  14.2 48.2 %all_to_all.15 = f32[512,4,128]{2,1,0:T(4,128)S(1)} all-to-all(f32[512,4,128]{2,1,0:T(4,128)S(1)} %copy.7), channel_id=1, replica_groups=mesh['x'=4,'yh'=4,'z'=8,'yl'=2,'core'=2] {'x','yh','z','yl','core'}, dimensions={0} | all-to-all | bytes 2097152 | tf_op jit(solution)/shard_map/all_to_all | solution.py:52
  62.5 0.5 reduce_sum.9
  63.0 1.1 broadcast_in_dim.36
  64.1 14.6 %all-to-all-start.2 = ((f32[512,4,128]{2,1,0:T(4,128)}), f32[512,4,128]{2,1,0:T(4,128)S(1)}, u32[]{:S(2)}, u32[]{:S(2)}) async-start(f32[512,4,128]{2,1,0:T(4,128)} %broadcast_in_dim.36), calls=%async_computation.2 | async-start | bytes 2097152 | tf_op jit(solution)/shard_map/all_to_all | solution.py:25
  78.7 0.0 copy-done.2
  78.7 0.0 copy-done.3
  78.8 27.2 %all-to-all-done.2 = f32[512,4,128]{2,1,0:T(4,128)S(1)} async-done(((f32[512,4,128]{2,1,0:T(4,128)}), f32[512,4,128]{2,1,0:T(4,128)S(1)}, u32[]{:S(2)}, u32[]{:S(2)}) %all-to-all-start.2) | async-done | bytes 1048608 | tf_op jit(solution)/shard_map/all_to_all | solution.py:25
  106.0 2.0 stack.2
  108.0 8.8 %all-to-all-start = ((f32[16,48,1024]{2,1,0:T(8,128)}), f32[16,48,1024]{2,1,0:T(8,128)S(1)}, u32[]{:S(2)}, u32[]{:S(2)}) async-start(f32[16,48,1024]{2,1,0:T(8,128)} %stack.2), calls=%async_computation | async-start | bytes 6291456 | tf_op jit(solution)/shard_map/all_to_all | solution.py:13
  116.8 0.2 all-gather.2.cloned.1.call-start
  117.0 0.6 pad_maximum_fusion.1
  117.6 0.0 all-gather.2.cloned.1.call-update
  117.7 2.6 %copy.8 = f32[512,4,128]{0,2,1:T(8,128)} copy(f32[512,4,128]{2,1,0:T(4,128)} %copy-done.1) | data formatting | bytes 2097152 | tf_op jit(solution)/shard_map/all_to_all | solution.py:25
  120.2 2.3 %bitcast_add_fusion = f32[512,512]{0,1:T(8,128)} fusion(f32[512,4,128]{0,2,1:T(8,128)} %copy.8, f32[512]{0:T(512)S(1)} %copy-done.6), kind=kLoop, calls=%fused_computation.14 | loop fusion | flops 786432 | bytes 2099200 | tf_op jit(solution)/shard_map/add | solution.py:58
  122.5 82.3 %all-gather.2.cloned.1.call-done = f32[512,1024]{1,0:T(8,128)} async-done(((f32[16,1024]{1,0:T(8,128)}), f32[512,1024]{1,0:T(8,128)}) %all-gather.2.cloned.1.call-update) | async-done | bytes 2097168 | tf_op jit(solution)/shard_map/all_gather | solution.py:55
  204.9 4.4 %fusion.9 = f32[512,512]{1,0:T(8,128)} fusion(f32[512,512]{0,1:T(8,128)} %bitcast_add_fusion, f32[512,1024]{1,0:T(8,128)} %all-gather.2.cloned.1.call-done), kind=kOutput, calls=%fused_computation.12 | convolution fusion | flops 1610612736 | bytes 3145728 | tf_op jit(solution)/shard_map/dot_general | solution.py:18
  209.3 0.0 all-to-all-done
  209.3 4.1 %fusion = f32[512,768]{1,0:T(8,128)S(1)} fusion(f32[512,512]{1,0:T(8,128)} %fusion.9, f32[768,1024]{1,0:T(8,128)S(1)} %bitcast.16), kind=kOutput, calls=%fused_computation | convolution fusion | flops 2415919104 | bytes 4194304 | tf_op jit(solution)/shard_map/dot_general | solution.py:18
  213.4 0.0 copy-done
  213.4 6.5 %convolution_add_fusion = f32[512,768]{1,0:T(8,128)} fusion(f32[512,768]{1,0:T(8,128)S(1)} %fusion, f32[512,1024]{1,0:T(8,128)S(1)} %copy-done, f32[768,1024]{1,0:T(8,128)S(1)} %bitcast.17), kind=kOutput, calls=%fused_computation.2 | convolution fusion | flops 4832231424 | bytes 8388608 | tf_op jit(solution)/shard_map/dot_general | solution.py:18
  (10 shorter events, 0.0 us)
Async XLA Ops:
  9.2 2.2 copy-start.4
  9.2 2.2 copy-start.5
  9.2 3.2 %copy-start.7 = (f32[512]{0:T(512)S(1)}, f32[512]{0:T(512)}, u32[]{:S(2)}) copy-start(f32[512]{0:T(512)} %param.10) | copy-start | bytes 6148
  62.5 16.2 %copy-start.2 = (f32[48,512]{1,0:T(8,128)S(1)}, f32[48,512]{1,0:T(8,128)}, u32[]{:S(2)}) copy-start(f32[48,512]{1,0:T(8,128)} %param.9) | copy-start | bytes 294916
  62.5 16.3 %copy-start.3 = (f32[48,512]{1,0:T(8,128)S(1)}, f32[48,512]{1,0:T(8,128)}, u32[]{:S(2)}) copy-start(f32[48,512]{1,0:T(8,128)} %param.8) | copy-start | bytes 294916
  64.1 41.8 %all-to-all-start.2 = ((f32[512,4,128]{2,1,0:T(4,128)}), f32[512,4,128]{2,1,0:T(4,128)S(1)}, u32[]{:S(2)}, u32[]{:S(2)}) async-start(f32[512,4,128]{2,1,0:T(4,128)} %broadcast_in_dim.36), calls=%async_computation.2 | async-start | bytes 2097152 | tf_op jit(solution)/shard_map/all_to_all | solution.py:25
  105.9 2.0 copy-start.1
  108.0 101.3 %all-to-all-start = ((f32[16,48,1024]{2,1,0:T(8,128)}), f32[16,48,1024]{2,1,0:T(8,128)S(1)}, u32[]{:S(2)}, u32[]{:S(2)}) async-start(f32[16,48,1024]{2,1,0:T(8,128)} %stack.2), calls=%async_computation | async-start | bytes 6291456 | tf_op jit(solution)/shard_map/all_to_all | solution.py:13
  116.8 3.5 %copy-start.6 = (f32[512]{0:T(512)S(1)}, f32[512]{0:T(512)}, u32[]{:S(2)}) copy-start(f32[512]{0:T(512)} %param.11) | copy-start | bytes 6148
  116.8 88.1 %all-gather.2.cloned.1.call-start = ((), (), s32[]{:S(2)}) async-start(), calls=%async_computation.3 | async-start | bytes 2162688 | tf_op jit(solution)/shard_map/all_gather | solution.py:55
  209.3 4.1 %copy-start = (f32[512,1024]{1,0:T(8,128)S(1)}, f32[512,1024]{1,0:T(8,128)}, u32[]{:S(2)}) copy-start(f32[512,1024]{1,0:T(8,128)} %all-gather.2.cloned.1.call-done) | copy-start | bytes 6291460
Sparse Core Ops, SparseCore 0:
  119.7 85.1 all-gather.1
